TPU v7x, 512 devices: a whole 4x4x16 slice. The times are simulated.
512 devices in a mesh: pipe: 4 (over z_lo), row: 16 (over x, z_hi), col: 8 (over y, core).
Axes of the slice: x: 4, y: 4, z: 16 (z_hi: 4, z_lo: 4; z = z_hi * 4 + z_lo), core: 2. Of those that a mesh axis runs over, the one named last changes fastest.
Arguments:
- saved_in: bfloat16 [4, 128, 128, 2048], P('pipe', 'row', 'col'), may hold values from -400 to 400
- cotangent: bfloat16 [4, 128, 128, 2048], P('pipe', 'row', 'col'), may hold values from -6 to 6
- section_gains: float32 [4, 5, 2048], P('pipe'), may hold values from -8 to 8
Outputs:
- next_grad: bfloat16 [4, 128, 128, 2048], P('pipe', 'row', 'col')
All inputs are finite; a program needn't handle non-finite values.
Results may differ from a plain program's by a relative error of at most 0.0028.
The roundings to bfloat16 on the way count: a program that leaves them out, or rounds other values in their place, can miss the bound.
Values may be sent and summed in bfloat16 or wider, within the bound.
A program may use at most 64 MiB of HBM per device.

v0:
```python
import functools
import math

import jax
import jax.numpy as jnp
from jax import lax
from jax.experimental import pallas as pl
from jax.experimental.pallas import tpu as pltpu
from jax.sharding import PartitionSpec as P

HEADS = 16
HEAD_DIM = 128
TILE = 8
SPAN = 5
REACH = SPAN // 2

NEGATIVE = -1e30
EPSILON = 1e-06
F32 = jnp.float32
BF16 = jnp.bfloat16


def dot(left, right, dims):
    return lax.dot_general(left, right, (dims, ((), ())), preferred_element_type=F32)


def fold(block, op):
    rows, lanes = block.shape
    return op(block.reshape(rows // 8, 8, lanes), axis=0)


def attention_kernel(
    x3_ref, r3_ref, cot_ref, gains_ref, own_ref, left_ref, right_ref,
    kv_ref, kt_ref, qd_ref, w_ref, st_ref, bias_ref,
):
    rows, area, depth = cot_ref.shape
    wide = 3 * area
    col = lax.axis_index("col")
    cols = lax.axis_size("col")
    gn = gains_ref[0:1, :]
    gq = gains_ref[1:2, :]
    gk = gains_ref[2:3, :]
    gv = gains_ref[3:4, :]
    go = gains_ref[4:5, :]

    key = lax.broadcasted_iota(jnp.int32, (wide, area), 0)
    query = lax.broadcasted_iota(jnp.int32, (wide, area), 1)
    key_tile = 2 * (key // area) + (key // TILE) % 2
    query_tile = (query // TILE) % 2
    near = (key_tile >= query_tile) & (key_tile <= query_tile + 2 * REACH)
    inside = (col * 2 + key_tile >= REACH) & (col * 2 + key_tile < 2 * cols + REACH)
    bias_ref[0] = jnp.full((wide, area), NEGATIVE, F32)
    bias_ref[1] = jnp.where(near & inside, 0.0, NEGATIVE)

    for pad in (0, 1, rows + 2, rows + 3):
        kv_ref[pad] = jnp.zeros((wide, 2 * depth), BF16)
        kt_ref[pad] = jnp.zeros((depth, wide), BF16)
        qd_ref[pad] = jnp.zeros((2 * area, 2 * depth), BF16)
    for key_row, slot in ((0, 0), (0, 1), (1, 0), (rows - 2, 4), (rows - 1, 3), (rows - 1, 4)):
        w_ref[key_row + REACH, :, slot * 2 * area : (slot + 1) * 2 * area] = jnp.zeros(
            (wide, 2 * area), BF16
        )

    def prepare(row, carry):
        for block in range(3):
            inverse = jnp.broadcast_to(r3_ref[block, pl.ds(row, 1), :], (area, area)).T
            x_float = x3_ref[block, row].astype(F32)
            normed = (x_float * inverse * gn).astype(BF16).astype(F32)
            keys = (normed * gk).astype(BF16)
            lanes = slice(block * area, (block + 1) * area)
            kv_ref[row + REACH, lanes, :depth] = keys
            kv_ref[row + REACH, lanes, depth:] = (normed * gv).astype(BF16)
            kt_ref[row + REACH, :, lanes] = keys.T
            if block == 1:
                qd_ref[row + REACH, :area, :depth] = (normed * gq).astype(BF16)
                qd_ref[row + REACH, :area, depth:] = jnp.zeros((area, depth), BF16)
                qd_ref[row + REACH, area:, :depth] = jnp.zeros((area, depth), BF16)
                qd_ref[row + REACH, area:, depth:] = (cot_ref[row].astype(F32) * go).astype(BF16)
        return carry

    lax.fori_loop(0, rows, prepare, 0)

    def query_row(row, carry):
        qd = qd_ref[row + REACH]
        top = jnp.full((8, area), NEGATIVE, F32)
        for off in range(SPAN):
            far = row + off - REACH
            valid = jnp.logical_and(far >= 0, far < rows).astype(jnp.int32)
            pair = dot(kv_ref[row + off], qd, ((1,), (1,)))
            scores = pair[:, :area] + bias_ref[valid]
            st_ref[off, :, :area] = scores
            st_ref[off, :, area:] = pair[:, area:]
            top = jnp.maximum(top, fold(scores, jnp.max))
        top = jnp.max(top, axis=0, keepdims=True)
        total = jnp.zeros((8, area), F32)
        for off in range(SPAN):
            raised = jnp.exp(st_ref[off, :, :area] - top)
            st_ref[off, :, :area] = raised
            total = total + fold(raised, jnp.sum)
        scale = 1.0 / jnp.sum(total, axis=0, keepdims=True)
        delta = jnp.zeros((8, area), F32)
        for off in range(SPAN):
            rounded = (st_ref[off, :, :area] * scale).astype(BF16)
            slot = SPAN - 1 - off
            w_ref[row + off, :, slot * 2 * area + area : (slot + 1) * 2 * area] = rounded
            delta = delta + fold(rounded.astype(F32) * st_ref[off, :, area:], jnp.sum)
        delta = jnp.sum(delta, axis=0, keepdims=True)
        turned = jnp.zeros((depth, area), F32)
        for off in range(SPAN):
            weights = st_ref[off, :, :area] * scale
            dscore = (weights * (st_ref[off, :, area:] - delta)).astype(BF16)
            slot = SPAN - 1 - off
            w_ref[row + off, :, slot * 2 * area : slot * 2 * area + area] = dscore
            turned = turned + dot(kt_ref[row + off], dscore, ((1,), (0,)))
        own_ref[row] = turned.T * gq
        return carry

    lax.fori_loop(0, rows, query_row, 0)

    def key_row(row, carry):
        queries = qd_ref[pl.ds(row, SPAN)].reshape(SPAN * 2 * area, 2 * depth)
        grads = dot(w_ref[row + REACH], queries, ((1,), (0,)))
        terms = grads[:, :depth] * gk + grads[:, depth:] * gv
        left_ref[row] = terms[:area]
        own_ref[row] = own_ref[row] + terms[area : 2 * area]
        right_ref[row] = terms[2 * area :]
        return carry

    lax.fori_loop(0, rows, key_row, 0)


def attention(x3, r3, cot, gains):
    rows, area, depth = cot.shape
    wide = 3 * area
    block = jax.ShapeDtypeStruct((rows, area, depth), F32)
    vmem = pl.BlockSpec(memory_space=pltpu.VMEM)
    return pl.pallas_call(
        attention_kernel,
        out_shape=(block, block, block),
        in_specs=[vmem] * 4,
        out_specs=(vmem, vmem, vmem),
        scratch_shapes=[
            pltpu.VMEM((rows + 4, wide, 2 * depth), BF16),
            pltpu.VMEM((rows + 4, depth, wide), BF16),
            pltpu.VMEM((rows + 4, 2 * area, 2 * depth), BF16),
            pltpu.VMEM((rows + 4, wide, SPAN * 2 * area), BF16),
            pltpu.VMEM((SPAN, wide, 2 * area), F32),
            pltpu.VMEM((2, wide, area), F32),
        ],
        compiler_params=pltpu.CompilerParams(vmem_limit_bytes=60 * 1024 * 1024),
        name="head_attention",
    )(x3, r3, cot, gains)


def shift(block, axis, distance):
    size = lax.axis_size(axis)
    route = [(i, i + distance) for i in range(size) if 0 <= i + distance < size]
    return lax.ppermute(block, axis, route)


def per_device(saved_in, cotangent, section_gains):
    _, tall, across, width = saved_in.shape
    area = tall * across
    factor = 1.0 / math.sqrt(HEAD_DIM)
    head = lax.axis_index("row")
    x = saved_in.reshape(area, width)
    cot = cotangent.reshape(area, width)
    x_float = x.astype(F32)
    inverse = lax.rsqrt(jnp.mean(x_float * x_float, axis=-1) + EPSILON)

    def by_head(block):
        return block.reshape(area, HEADS, HEAD_DIM).transpose(1, 0, 2)

    packed = jnp.stack([by_head(x), by_head(cot)], axis=1)
    packed = lax.all_to_all(packed, "row", 0, 0)
    inverse = lax.all_gather(inverse, "row")
    x_head = packed[:, 0]
    cot_head = packed[:, 1]
    x3 = jnp.stack([shift(x_head, "col", 1), x_head, shift(x_head, "col", -1)])
    r3 = jnp.stack([shift(inverse, "col", 1), inverse, shift(inverse, "col", -1)])
    gains = lax.dynamic_slice_in_dim(section_gains[0], head * HEAD_DIM, HEAD_DIM, 1)
    gains = gains * jnp.array([1.0, factor, 1.0, 1.0, 1.0], F32)[:, None]
    gains = jnp.concatenate([gains, jnp.zeros((3, HEAD_DIM), F32)], axis=0)
    own, left, right = attention(x3, r3, cot_head, gains)
    dnormed = own + shift(left, "col", -1) + shift(right, "col", 1)
    scaled = dnormed * gains[0]
    x_head = x_head.astype(F32)
    mean = lax.psum(jnp.sum(x_head * scaled, axis=-1), "row") / width
    inv = inverse[..., None]
    grad = cot_head.astype(F32) + inv * scaled - x_head * (inv * inv * inv) * mean[..., None]
    grad = lax.all_to_all(grad.astype(BF16), "row", 0, 0)
    grad = grad.transpose(1, 0, 2).reshape(1, tall, across, width)
    return shift(grad, "pipe", -1)


def solution(mesh):
    return jax.shard_map(
        per_device,
        mesh=mesh,
        in_specs=(
            P("pipe", "row", "col", None),
            P("pipe", "row", "col", None),
            P("pipe", None, None),
        ),
        out_specs=P("pipe", "row", "col", None),
        check_vma=False,
    )
```

profile of v0, /device:TPU:16, one launch (start us, length us, event | category | flops | bytes accessed | tf_op | source)
XLA Modules:
  0.0 296.0 jit_solution(716538477501023145)
XLA Ops:
  0.0 0.0 copy-start
  0.0 1.1 copy.18
  1.2 1.1 copy.17
  2.3 0.1 pad_maximum_fusion.1
  2.4 0.0 copy-start.1
  2.4 1.2 copy.10
  3.7 17.7 %all-to-all-start = ((bf16[16,2,128,128]{3,2,1,0:T(8,128)(2,1)}), bf16[16,2,128,128]{3,2,1,0:T(8,128)(2,1)S(1)}, u32[]{:S(2)}, u32[]{:S(2)}) async-start(bf16[16,2,128,128]{3,2,1,0:T(8,128)(2,1)} %copy.10), calls=%async_computation | async-start | bytes 2097152 | tf_op jit(solution)/shard_map/all_to_all | solution.py:175
  21.3 0.0 copy-done.1
  21.4 0.0 copy-start.2
  21.4 0.2 multiply_reduce_fusion
  21.5 49.7 %all-to-all-done = bf16[16,2,128,128]{3,2,1,0:T(8,128)(2,1)S(1)} async-done(((bf16[16,2,128,128]{3,2,1,0:T(8,128)(2,1)}), bf16[16,2,128,128]{3,2,1,0:T(8,128)(2,1)S(1)}, u32[]{:S(2)}, u32[]{:S(2)}) %all-to-all-start) | async-done | bytes 1048608 | tf_op jit(solution)/shard_map/all_to_all | solution.py:175
  71.2 1.1 slice_bitcast_fusion
  72.3 1.9 collective-permute-start.1
  74.2 2.4 collective-permute-start
  76.6 0.1 reshape.36
  76.7 50.3 %all-gather = f32[16,1,128]{2,1,0:T(1,128)S(1)} all-gather(f32[1,1,128]{2,1,0:T(1,128)S(1)} %reshape.36), channel_id=1, replica_groups=mesh['pipe'=4,'row'=16,'col'=8] {'row'}, dimensions={0}, use_global_device_ids=true | all-gather | bytes 8704 | tf_op jit(solution)/shard_map/all_gather | solution.py:176
  127.0 1.9 collective-permute-start.3
  129.0 2.4 collective-permute-start.2
  131.4 0.0 copy-done
  131.4 0.0 copy-done.2
  131.4 0.1 bitcast_multiply_fusion
  131.5 0.6 concatenate.3.gains_ref
  132.1 0.0 collective-permute-done.3
  132.1 1.8 collective-permute-done.2
  133.9 0.6 pad_maximum_fusion.2.r3_ref
  134.5 0.0 collective-permute-done.1
  134.5 0.0 collective-permute-done
  134.5 1.3 pad_maximum_fusion.x3_ref
  135.9 37.7 %head_attention.1 = (f32[16,128,128]{2,1,0:T(8,128)}, f32[16,128,128]{2,1,0:T(8,128)}, f32[16,128,128]{2,1,0:T(8,128)}) custom-call(bf16[3,16,128,128]{3,2,1,0:T(8,128)(2,1)} %pad_maximum_fusion.x3_ref, f32[3,16,128]{2,1,0:T(8,128)} %pad_maximum_fusion.2.r3_ref, bf16[16,128,128]{2,1,0:T(8,128)(2,1)} %get-tuple-element.13.cot_ref, f32[8,128]{1,0:T(8,128)} %concatenate.3.gains_ref), custom_call_target="tpu_custom_call" | custom-call | tf_op jit(solution)/shard_map/head_attention/pallas_call | solution.py:137
  173.6 1.9 collective-permute-start.5
  175.5 3.6 %collective-permute-start.4 = (f32[16,128,128]{2,1,0:T(8,128)}, f32[16,128,128]{2,1,0:T(8,128)S(1)}, u32[]{:S(2)}, u32[]{:S(2)}) collective-permute-start(f32[16,128,128]{2,1,0:T(8,128)} %get-tuple-element.9), channel_id=1, source_target_pairs={{1,0},{2,1},{3,2},{4,3},{5,4},{6,5},{7,6},{9,8},{10,9},{11,10},{12... | collective-permute-start | bytes 3145736 | tf_op jit(solution)/shard_map/ppermute | solution.py:158
  179.2 10.7 %collective-permute-done.5 = f32[16,128,128]{2,1,0:T(8,128)S(1)} collective-permute-done((f32[16,128,128]{2,1,0:T(8,128)}, f32[16,128,128]{2,1,0:T(8,128)S(1)}, u32[]{:S(2)}, u32[]{:S(2)}) %collective-permute-start.5) | collective-permute-done | bytes 1048608 | tf_op jit(solution)/shard_map/ppermute | solution.py:158
  189.9 1.9 collective-permute-done.4
  191.8 1.6 fusion.3
  193.4 49.2 %psum.7 = f32[16,128]{1,0:T(8,128)S(1)} all-reduce(f32[16,128]{1,0:T(8,128)S(1)} %get-tuple-element.11), channel_id=1, replica_groups=mesh['pipe'=4,'row'=16,'col'=8] {'row'}, use_global_device_ids=true, to_apply=%region_2.0 | all-reduce | flops 2048 | bytes 16384 | tf_op jit(solution)/shard_map/psum | solution.py:188
  242.6 1.0 fusion.2
  243.6 32.4 %all_to_all.10 = bf16[16,128,128]{2,1,0:T(8,128)(2,1)S(1)} all-to-all(bf16[16,128,128]{2,1,0:T(8,128)(2,1)S(1)} %fusion.2), channel_id=1, replica_groups=mesh['pipe'=4,'row'=16,'col'=8] {'row'}, dimensions={0} | all-to-all | bytes 1048576 | tf_op jit(solution)/shard_map/all_to_all | solution.py:191
  276.0 0.3 copy.13
  276.3 0.2 reshape.35
  276.6 1.3 collective-permute-start.6
  277.9 17.3 %collective-permute-done.6 = bf16[1,8,16,2048]{3,2,1,0:T(8,128)(2,1)S(1)} collective-permute-done((bf16[1,8,16,2048]{3,2,1,0:T(8,128)(2,1)S(1)}, bf16[1,8,16,2048]{3,2,1,0:T(8,128)(2,1)S(1)}, u32[]{:S(2)}, u32[]{:S(2)}) %collective-permute-start.6) | collective-permute-done | bytes 524320 | tf_op jit(solution)/shard_map/ppermute | solution.py:158
  295.2 0.8 copy.21
  (5 shorter events, 0.0 us)
Async XLA Ops:
  0.0 131.4 %copy-start = (f32[1,5,2048]{2,0,1:T(1,128)S(1)}, f32[1,5,2048]{2,0,1:T(1,128)}, u32[]{:S(2)}) copy-start(f32[1,5,2048]{2,0,1:T(1,128)} %param.6) | copy-start | bytes 122884
  2.4 18.9 %copy-start.1 = (bf16[1,8,16,2048]{3,2,1,0:T(8,128)(2,1)S(1)}, bf16[1,8,16,2048]{3,2,1,0:T(8,128)(2,1)}, u32[]{:S(2)}) copy-start(bf16[1,8,16,2048]{3,2,1,0:T(8,128)(2,1)} %param.4) | copy-start | bytes 1572868
  3.7 67.6 %all-to-all-start = ((bf16[16,2,128,128]{3,2,1,0:T(8,128)(2,1)}), bf16[16,2,128,128]{3,2,1,0:T(8,128)(2,1)S(1)}, u32[]{:S(2)}, u32[]{:S(2)}) async-start(bf16[16,2,128,128]{3,2,1,0:T(8,128)(2,1)} %copy.10), calls=%async_computation | async-start | bytes 2097152 | tf_op jit(solution)/shard_map/all_to_all | solution.py:175
  21.4 110.0 %copy-start.2 = (f32[5]{0:T(128)S(1)}, f32[5]{0:T(128)}, u32[]{:S(2)}) copy-start(f32[5]{0:T(128)} %constant.25.clone) | copy-start | bytes 64
  72.3 62.2 %collective-permute-start.1 = (bf16[16,128,128]{2,1,0:T(8,128)(2,1)S(1)}, bf16[16,128,128]{2,1,0:T(8,128)(2,1)S(1)}, u32[]{:S(2)}, u32[]{:S(2)}) collective-permute-start(bf16[16,128,128]{2,1,0:T(8,128)(2,1)S(1)} %get-tuple-element.14), channel_id=1, source_target_pairs={{1,0},{2,1},{3,2},{4,3},{5,4},{6,5},{7,6},{9,8},{10,9},{11,10},{12... | collective-permute-start | bytes 1572872 | tf_op jit(solution)/shard_map/ppermute | solution.py:158
  74.2 60.3 %collective-permute-start = (bf16[16,128,128]{2,1,0:T(8,128)(2,1)S(1)}, bf16[16,128,128]{2,1,0:T(8,128)(2,1)S(1)}, u32[]{:S(2)}, u32[]{:S(2)}) collective-permute-start(bf16[16,128,128]{2,1,0:T(8,128)(2,1)S(1)} %get-tuple-element.14), channel_id=1, source_target_pairs={{0,1},{1,2},{2,3},{3,4},{4,5},{5,6},{6,7},{8,9},{9,10},{10,11},{11... | collective-permute-start | bytes 1572872 | tf_op jit(solution)/shard_map/ppermute | solution.py:158
  127.0 5.0 %collective-permute-start.3 = (f32[16,128]{1,0:T(8,128)S(1)}, f32[16,128]{1,0:T(8,128)S(1)}, u32[]{:S(2)}, u32[]{:S(2)}) collective-permute-start(f32[16,128]{1,0:T(8,128)S(1)} %bitcast.51), channel_id=1, source_target_pairs={{1,0},{2,1},{3,2},{4,3},{5,4},{6,5},{7,6},{9,8},{10,9},{11,10},{12... | collective-permute-start | bytes 24584 | tf_op jit(solution)/shard_map/ppermute | solution.py:158
  129.0 5.0 %collective-permute-start.2 = (f32[16,128]{1,0:T(8,128)S(1)}, f32[16,128]{1,0:T(8,128)S(1)}, u32[]{:S(2)}, u32[]{:S(2)}) collective-permute-start(f32[16,128]{1,0:T(8,128)S(1)} %bitcast.52), channel_id=1, source_target_pairs={{0,1},{1,2},{2,3},{3,4},{4,5},{5,6},{6,7},{8,9},{9,10},{10,11},{11... | collective-permute-start | bytes 24584 | tf_op jit(solution)/shard_map/ppermute | solution.py:158
  173.6 16.3 %collective-permute-start.5 = (f32[16,128,128]{2,1,0:T(8,128)}, f32[16,128,128]{2,1,0:T(8,128)S(1)}, u32[]{:S(2)}, u32[]{:S(2)}) collective-permute-start(f32[16,128,128]{2,1,0:T(8,128)} %get-tuple-element.10), channel_id=1, source_target_pairs={{0,1},{1,2},{2,3},{3,4},{4,5},{5,6},{6,7},{8,9},{9,10},{10,11},{11... | collective-permute-start | bytes 3145736 | tf_op jit(solution)/shard_map/ppermute | solution.py:158
  175.5 16.3 %collective-permute-start.4 = (f32[16,128,128]{2,1,0:T(8,128)}, f32[16,128,128]{2,1,0:T(8,128)S(1)}, u32[]{:S(2)}, u32[]{:S(2)}) collective-permute-start(f32[16,128,128]{2,1,0:T(8,128)} %get-tuple-element.9), channel_id=1, source_target_pairs={{1,0},{2,1},{3,2},{4,3},{5,4},{6,5},{7,6},{9,8},{10,9},{11,10},{12... | collective-permute-start | bytes 3145736 | tf_op jit(solution)/shard_map/ppermute | solution.py:158
  276.6 18.6 %collective-permute-start.6 = (bf16[1,8,16,2048]{3,2,1,0:T(8,128)(2,1)S(1)}, bf16[1,8,16,2048]{3,2,1,0:T(8,128)(2,1)S(1)}, u32[]{:S(2)}, u32[]{:S(2)}) collective-permute-start(bf16[1,8,16,2048]{3,2,1,0:T(8,128)(2,1)S(1)} %reshape.35), channel_id=1, source_target_pairs={{128,0},{256,128},{384,256},{129,1},{257,129},{385,257},{130,2},{2... | collective-permute-start | bytes 1572872 | tf_op jit(solution)/shard_map/ppermute | solution.py:158
where the time goes:
time: 297 us; the launch traced here: 296 us
  blocking collectives  132 us (44%)
  waiting for transfers between devices  81.5 us (27%)
  Pallas kernels  37.7 us (13%)
  starting transfers between devices  33.1 us (11%)
  local copies, waits for them, and re-layouts  6.68 us (2%)
  other arithmetic  4.91 us (2%)
    all_gather x1, blocking collectives, per_device(): inverse = lax.all_gather(inverse, 'row')  50.3 us
    all_to_all x1, waiting for transfers between devices, per_device(): packed = lax.all_to_all(packed, 'row', 0, 0)  49.7 us
    psum x1, blocking collectives, per_device(): mean = lax.psum(jnp.sum(x_head * scaled, axis=-1), 'row') / width  49.2 us
    pallas_call x1, Pallas kernels, attention(): pl.pallas_call(attention_kernel, out_shape=(block, block, block), in_spec...  37.7 us
    all_to_all x1, blocking collectives, per_device(): grad = lax.all_to_all(grad.astype(BF16), 'row', 0, 0)  32.4 us
    ppermute x7, waiting for transfers between devices, shift(): return lax.ppermute(block, axis, route)  31.8 us
    all_to_all x1, starting transfers between devices, per_device(): packed = lax.all_to_all(packed, 'row', 0, 0)  17.7 us
    ppermute x7, starting transfers between devices, shift(): return lax.ppermute(block, axis, route)  15.5 us
  transfers between devices with their start and end apart: 8, of which 5 were waited for; matrix products, arithmetic and copies ran while one was open for 1% of the time, Pallas kernels for 0%

commit v1 on v0

--- a/solution.py
+++ b/solution.py
@@ -1,4 +1,3 @@
-import functools
 import math
 
 import jax
@@ -18,6 +17,7 @@
 EPSILON = 1e-06
 F32 = jnp.float32
 BF16 = jnp.bfloat16
+MESH = pl.DeviceIdType.MESH
 
 
 def dot(left, right, dims):
@@ -29,7 +29,18 @@
     return op(block.reshape(rows // 8, 8, lanes), axis=0)
 
 
-def attention_kernel(
+def head_gains(gains_ref):
+    start = pl.multiple_of(lax.axis_index("row") * HEAD_DIM, HEAD_DIM)
+    return gains_ref[:, pl.ds(start, HEAD_DIM)]
+
+
+def attention_kernel(*refs):
+    @pl.when(lax.axis_index("pipe") > 0)
+    def _():
+        attention_body(*refs)
+
+
+def attention_body(
     x3_ref, r3_ref, cot_ref, gains_ref, own_ref, left_ref, right_ref,
     kv_ref, kt_ref, qd_ref, w_ref, st_ref, bias_ref,
 ):
@@ -37,11 +48,12 @@
     wide = 3 * area
     col = lax.axis_index("col")
     cols = lax.axis_size("col")
-    gn = gains_ref[0:1, :]
-    gq = gains_ref[1:2, :]
-    gk = gains_ref[2:3, :]
-    gv = gains_ref[3:4, :]
-    go = gains_ref[4:5, :]
+    gains = head_gains(gains_ref)
+    gn = gains[0:1, :]
+    gq = gains[1:2, :] * (1.0 / math.sqrt(HEAD_DIM))
+    gk = gains[2:3, :]
+    gv = gains[3:4, :]
+    go = gains[4:5, :]
 
     key = lax.broadcasted_iota(jnp.int32, (wide, area), 0)
     query = lax.broadcasted_iota(jnp.int32, (wide, area), 1)
@@ -63,9 +75,12 @@
 
     def prepare(row, carry):
         for block in range(3):
-            inverse = jnp.broadcast_to(r3_ref[block, pl.ds(row, 1), :], (area, area)).T
+            inverse = jnp.broadcast_to(r3_ref[block, row, 0:1, :], (area, area)).T
             x_float = x3_ref[block, row].astype(F32)
             normed = (x_float * inverse * gn).astype(BF16).astype(F32)
+            if block != 1:
+                present = col > 0 if block == 0 else col < cols - 1
+                normed = jnp.where(present, normed, 0.0)
             keys = (normed * gk).astype(BF16)
             lanes = slice(block * area, (block + 1) * area)
             kv_ref[row + REACH, lanes, :depth] = keys
@@ -152,45 +167,431 @@
     )(x3, r3, cot, gains)
 
 
-def shift(block, axis, distance):
-    size = lax.axis_size(axis)
-    route = [(i, i + distance) for i in range(size) if 0 <= i + distance < size]
-    return lax.ppermute(block, axis, route)
+def greet(devices):
+    barrier = pltpu.get_barrier_semaphore()
+    for device in devices:
+        pl.semaphore_signal(barrier, inc=1, device_id=device, device_id_type=MESH)
+
+
+def greet_rows(others):
+    barrier = pltpu.get_barrier_semaphore()
+    me = lax.axis_index("row")
+
+    def step(hop, carry):
+        pl.semaphore_signal(
+            barrier, inc=1, device_id={"row": lax.rem(me + hop, HEADS)}, device_id_type=MESH
+        )
+        return carry
+
+    lax.fori_loop(1, others + 1, step, 0)
+
+
+def head_lanes(head):
+    return pl.ds(pl.multiple_of(head * HEAD_DIM, HEAD_DIM), HEAD_DIM)
+
+
+def remote(src, dst, send, recv, device):
+    return pltpu.make_async_remote_copy(
+        src_ref=src, dst_ref=dst, send_sem=send, recv_sem=recv,
+        device_id=device, device_id_type=MESH,
+    )
+
+
+def gather_kernel(*refs):
+    @pl.when(lax.axis_index("pipe") > 0)
+    def _():
+        gather_body(*refs)
+
+
+def gather_body(
+    x_ref, x_far, cot_far, x3_ref, r3_ref, cot_ref, inv_ref,
+    local_sem, x_send, x_recv, r_send, r_recv, c_send, c_recv,
+    fx_send, fx_recv, fr_send, fr_recv,
+):
+    me = lax.axis_index("row")
+    col = lax.axis_index("col")
+    cols = lax.axis_size("col")
+    area = x_ref.shape[0]
+    barrier = pltpu.get_barrier_semaphore()
+    greet_rows(HEADS - 1)
+
+    @pl.when(col > 0)
+    def _():
+        greet([{"col": col - 1}])
+
+    @pl.when(col < cols - 1)
+    def _():
+        greet([{"col": col + 1}])
+
+    own_x = pltpu.make_async_copy(x_far.at[:, head_lanes(me)], x3_ref.at[1, me], local_sem.at[0])
+    own_c = pltpu.make_async_copy(cot_far.at[:, head_lanes(me)], cot_ref.at[me], local_sem.at[1])
+    own_x.start()
+    own_c.start()
+    x_float = x_ref[...].astype(F32)
+    square = jnp.mean(x_float * x_float, axis=-1, keepdims=True)
+    inverse = jnp.broadcast_to(lax.rsqrt(square + EPSILON), (area, area))
+    inv_ref[...] = inverse.T[:8]
+    own_r = pltpu.make_async_copy(inv_ref, r3_ref.at[1, me], local_sem.at[2])
+    pl.semaphore_wait(
+        barrier, HEADS - 1 + (col > 0).astype(jnp.int32) + (col < cols - 1).astype(jnp.int32)
+    )
+
+    def x_copy(src, dst):
+        return remote(
+            x_far.at[:, head_lanes(dst)], x3_ref.at[1, src], x_send.at[dst], x_recv.at[src],
+            {"row": dst},
+        )
+
+    def r_copy(src, dst):
+        return remote(inv_ref, r3_ref.at[1, src], r_send.at[dst], r_recv.at[src], {"row": dst})
+
+    def c_copy(src, dst):
+        return remote(
+            cot_far.at[:, head_lanes(dst)], cot_ref.at[src], c_send.at[dst], c_recv.at[src],
+            {"row": dst},
+        )
+
+    def to(hop):
+        return lax.rem(me + hop, HEADS)
+
+    def back(hop):
+        return lax.rem(me + HEADS - hop, HEADS)
+
+    def start_x(hop, carry):
+        x_copy(me, to(hop)).start()
+        return carry
+
+    def start_rest(hop, carry):
+        c_copy(me, to(hop)).start()
+        return carry
+
+    def start_r(hop, carry):
+        r_copy(me, to(hop)).start()
+        return carry
+
+    lax.fori_loop(1, HEADS, start_x, 0)
+    lax.fori_loop(1, HEADS, start_r, 0)
+    own_r.start()
+    lax.fori_loop(1, HEADS, start_rest, 0)
+
+    def beside(src, side):
+        device = {"col": col - 1} if side == 0 else {"col": col + 1}
+        slot = 2 - 2 * side
+        return (
+            remote(
+                x3_ref.at[1, src], x3_ref.at[slot, src], fx_send.at[side, src],
+                fx_recv.at[side, src], device,
+            ),
+            remote(
+                r3_ref.at[1, src], r3_ref.at[slot, src], fr_send.at[side, src],
+                fr_recv.at[side, src], device,
+            ),
+        )
+
+    def forward(src):
+        @pl.when(col > 0)
+        def _():
+            for copy in beside(src, 0):
+                copy.start()
+
+        @pl.when(col < cols - 1)
+        def _():
+            for copy in beside(src, 1):
+                copy.start()
+
+    own_x.wait()
+    own_r.wait()
+    forward(me)
+
+    def pass_on(hop, carry):
+        src = back(hop)
+        x_copy(src, me).wait_recv()
+        r_copy(src, me).wait_recv()
+        forward(src)
+        return carry
+
+    lax.fori_loop(1, HEADS, pass_on, 0)
+
+    def finish(hop, carry):
+        x_copy(me, to(hop)).wait_send()
+        r_copy(me, to(hop)).wait_send()
+        c_copy(me, to(hop)).wait_send()
+        c_copy(back(hop), me).wait_recv()
+        return carry
+
+    lax.fori_loop(1, HEADS, finish, 0)
+    own_c.wait()
+
+    def finish_beside(src, carry):
+        @pl.when(col > 0)
+        def _():
+            for copy in beside(src, 0):
+                copy.wait_send()
+            for copy in beside(src, 1):
+                copy.wait_recv()
+
+        @pl.when(col < cols - 1)
+        def _():
+            for copy in beside(src, 1):
+                copy.wait_send()
+            for copy in beside(src, 0):
+                copy.wait_recv()
+
+        return carry
+
+    lax.fori_loop(0, HEADS, finish_beside, 0)
+
+
+def gather(x, cot):
+    area = x.shape[0]
+    far = pl.BlockSpec(memory_space=pl.ANY)
+    vmem = pl.BlockSpec(memory_space=pltpu.VMEM)
+    dma = pltpu.SemaphoreType.DMA
+    return pl.pallas_call(
+        gather_kernel,
+        out_shape=(
+            jax.ShapeDtypeStruct((3, HEADS, area, HEAD_DIM), BF16),
+            jax.ShapeDtypeStruct((3, HEADS, 8, area), F32),
+            jax.ShapeDtypeStruct((HEADS, area, HEAD_DIM), BF16),
+        ),
+        in_specs=[vmem, far, far],
+        out_specs=(far, far, far),
+        scratch_shapes=[
+            pltpu.VMEM((8, area), F32),
+            dma((3,)),
+            dma((HEADS,)), dma((HEADS,)), dma((HEADS,)), dma((HEADS,)), dma((HEADS,)), dma((HEADS,)),
+            dma((2, HEADS)), dma((2, HEADS)), dma((2, HEADS)), dma((2, HEADS)),
+        ],
+        compiler_params=pltpu.CompilerParams(collective_id=0, has_side_effects=True),
+        name="gather_heads",
+    )(x, x, cot)
+
+
+PARTS = 4
+
+
+def scatter_kernel(
+    own_ref, left_far, right_far, x3_far, r3_far, cot_ref, gains_ref, out_ref,
+    x_ref, r_ref, from_ref, scaled_ref, mean_ref, means_ref, grad_ref,
+    local_sem, t_send, t_recv, m_send, m_recv, g_send, g_recv,
+):
+    me = lax.axis_index("row")
+    col = lax.axis_index("col")
+    cols = lax.axis_size("col")
+    pipe = lax.axis_index("pipe")
+    pipes = lax.axis_size("pipe")
+    rows, area, depth = own_ref.shape
+    width = rows * depth
+    span = rows // PARTS
+    barrier = pltpu.get_barrier_semaphore()
+
+    def grad_copy(src, dst):
+        return remote(
+            grad_ref.at[dst], out_ref.at[:, head_lanes(src)], g_send.at[dst], g_recv.at[src],
+            {"pipe": pipe - 1, "row": dst},
+        )
+
+    @pl.when(pipe < pipes - 1)
+    def _():
+        def step(row, carry):
+            pl.semaphore_signal(
+                barrier, inc=1, device_id={"pipe": pipe + 1, "row": row}, device_id_type=MESH
+            )
+            return carry
+
+        lax.fori_loop(0, rows, step, 0)
+
+    @pl.when(pipe > 0)
+    def _():
+        greet_rows(HEADS - 1)
+
+        @pl.when(col > 0)
+        def _():
+            greet([{"col": col - 1}])
+
+        @pl.when(col < cols - 1)
+        def _():
+            greet([{"col": col + 1}])
+
+        load_x = pltpu.make_async_copy(x3_far.at[1], x_ref, local_sem.at[0])
+        load_r = pltpu.make_async_copy(r3_far.at[1], r_ref, local_sem.at[1])
+        load_x.start()
+        load_r.start()
+        gains = head_gains(gains_ref)
+        gn = gains[0:1, :]
+        pl.semaphore_wait(
+            barrier, 2 * HEADS - 1 + (col > 0).astype(jnp.int32) + (col < cols - 1).astype(jnp.int32)
+        )
+
+        def term_copy(side, part):
+            lines = pl.ds(part * span, span)
+            return remote(
+                (left_far if side == 0 else right_far).at[lines], from_ref.at[side, lines],
+                t_send.at[side, part], t_recv.at[side, part],
+                {"col": col - 1} if side == 0 else {"col": col + 1},
+            )
+
+        for part in range(PARTS):
+            @pl.when(col > 0)
+            def _():
+                term_copy(0, part).start()
+
+            @pl.when(col < cols - 1)
+            def _():
+                term_copy(1, part).start()
+
+        load_x.wait()
+        load_r.wait()
+        for part in range(PARTS):
+            @pl.when(col < cols - 1)
+            def _():
+                term_copy(0, part).wait_recv()
+
+            @pl.when(col > 0)
+            def _():
+                term_copy(1, part).wait_recv()
+
+            def total(row, carry):
+                dnormed = own_ref[row]
+                dnormed = dnormed + jnp.where(col < cols - 1, from_ref[0, row], 0.0)
+                dnormed = dnormed + jnp.where(col > 0, from_ref[1, row], 0.0)
+                scaled = dnormed * gn
+                scaled_ref[row] = scaled
+                product = (x_ref[row].astype(F32) * scaled).T
+                mean_ref[pl.ds(row, 1), :] = jnp.sum(product, axis=0, keepdims=True)
+                return carry
+
+            lax.fori_loop(part * span, (part + 1) * span, total, 0)
+
+        def mean_copy(src, dst):
+            return remote(
+                mean_ref, means_ref.at[src], m_send.at[dst], m_recv.at[src], {"row": dst}
+            )
+
+        def to(hop):
+            return lax.rem(me + hop, HEADS)
+
+        def back(hop):
+            return lax.rem(me + HEADS - hop, HEADS)
+
+        def start_mean(hop, carry):
+            mean_copy(me, to(hop)).start()
+            return carry
+
+        def wait_mean(hop, carry):
+            mean_copy(back(hop), me).wait_recv()
+            return carry
+
+        lax.fori_loop(1, HEADS, start_mean, 0)
+        means_ref[me] = mean_ref[...]
+        lax.fori_loop(1, HEADS, wait_mean, 0)
+        mean_all = jnp.sum(means_ref[...], axis=0) / width
+        means_ref[0] = mean_all
+
+        def finish(row, carry):
+            inverse = jnp.broadcast_to(r_ref[row, 0:1, :], (area, area))
+            cube = inverse * inverse * inverse
+            pull = (cube * means_ref[0, pl.ds(row, 1), :]).T
+            grad = (
+                cot_ref[row].astype(F32)
+                + inverse.T * scaled_ref[row]
+                - x_ref[row].astype(F32) * pull
+            )
+            grad_ref[row] = grad.astype(BF16)
+
+            @pl.when(row > 0)
+            def _():
+                grad_copy(me, row - 1).start()
+
+            return carry
+
+        lax.fori_loop(0, rows, finish, 0)
+        grad_copy(me, rows - 1).start()
+
+    @pl.when(pipe == pipes - 1)
+    def _():
+        out_ref[...] = jnp.zeros_like(out_ref)
+
+    @pl.when(pipe < pipes - 1)
+    def _():
+        def wait_grad(row, carry):
+            remote(
+                grad_ref.at[0], out_ref.at[:, head_lanes(row)], g_send.at[0], g_recv.at[row],
+                {"pipe": pipe + 1, "row": row},
+            ).wait_recv()
+            return carry
+
+        lax.fori_loop(0, rows, wait_grad, 0)
+
+    @pl.when(pipe > 0)
+    def _():
+        def drain(row, carry):
+            grad_copy(me, row).wait_send()
+            return carry
+
+        lax.fori_loop(0, rows, drain, 0)
+
+        def drain_mean(hop, carry):
+            dst = lax.rem(me + hop, HEADS)
+            remote(
+                mean_ref, means_ref.at[me], m_send.at[dst], m_recv.at[me], {"row": dst}
+            ).wait_send()
+            return carry
+
+        lax.fori_loop(1, HEADS, drain_mean, 0)
+        for part in range(PARTS):
+            lines = pl.ds(part * span, span)
+
+            @pl.when(col > 0)
+            def _():
+                remote(
+                    left_far.at[lines], from_ref.at[0, lines], t_send.at[0, part],
+                    t_recv.at[0, part], {"col": col - 1},
+                ).wait_send()
+
+            @pl.when(col < cols - 1)
+            def _():
+                remote(
+                    right_far.at[lines], from_ref.at[1, lines], t_send.at[1, part],
+                    t_recv.at[1, part], {"col": col + 1},
+                ).wait_send()
+
+
+def scatter(own, left, right, x3, r3, cot, gains):
+    rows, area, depth = own.shape
+    far = pl.BlockSpec(memory_space=pl.ANY)
+    vmem = pl.BlockSpec(memory_space=pltpu.VMEM)
+    dma = pltpu.SemaphoreType.DMA
+    return pl.pallas_call(
+        scatter_kernel,
+        out_shape=jax.ShapeDtypeStruct((area, rows * depth), BF16),
+        in_specs=[vmem, far, far, far, far, vmem, vmem],
+        out_specs=vmem,
+        scratch_shapes=[
+            pltpu.VMEM((rows, area, depth), BF16),
+            pltpu.VMEM((rows, 8, area), F32),
+            pltpu.VMEM((2, rows, area, depth), F32),
+            pltpu.VMEM((rows, area, depth), F32),
+            pltpu.VMEM((rows, area), F32),
+            pltpu.VMEM((HEADS, rows, area), F32),
+            pltpu.VMEM((rows, area, depth), BF16),
+            dma((2,)),
+            dma((2, PARTS)), dma((2, PARTS)),
+            dma((HEADS,)), dma((HEADS,)), dma((HEADS,)), dma((HEADS,)),
+        ],
+        compiler_params=pltpu.CompilerParams(collective_id=1, has_side_effects=True),
+        name="finish_and_return",
+    )(own, left, right, x3, r3, cot, gains)
 
 
 def per_device(saved_in, cotangent, section_gains):
     _, tall, across, width = saved_in.shape
     area = tall * across
-    factor = 1.0 / math.sqrt(HEAD_DIM)
-    head = lax.axis_index("row")
-    x = saved_in.reshape(area, width)
-    cot = cotangent.reshape(area, width)
-    x_float = x.astype(F32)
-    inverse = lax.rsqrt(jnp.mean(x_float * x_float, axis=-1) + EPSILON)
-
-    def by_head(block):
-        return block.reshape(area, HEADS, HEAD_DIM).transpose(1, 0, 2)
-
-    packed = jnp.stack([by_head(x), by_head(cot)], axis=1)
-    packed = lax.all_to_all(packed, "row", 0, 0)
-    inverse = lax.all_gather(inverse, "row")
-    x_head = packed[:, 0]
-    cot_head = packed[:, 1]
-    x3 = jnp.stack([shift(x_head, "col", 1), x_head, shift(x_head, "col", -1)])
-    r3 = jnp.stack([shift(inverse, "col", 1), inverse, shift(inverse, "col", -1)])
-    gains = lax.dynamic_slice_in_dim(section_gains[0], head * HEAD_DIM, HEAD_DIM, 1)
-    gains = gains * jnp.array([1.0, factor, 1.0, 1.0, 1.0], F32)[:, None]
-    gains = jnp.concatenate([gains, jnp.zeros((3, HEAD_DIM), F32)], axis=0)
-    own, left, right = attention(x3, r3, cot_head, gains)
-    dnormed = own + shift(left, "col", -1) + shift(right, "col", 1)
-    scaled = dnormed * gains[0]
-    x_head = x_head.astype(F32)
-    mean = lax.psum(jnp.sum(x_head * scaled, axis=-1), "row") / width
-    inv = inverse[..., None]
-    grad = cot_head.astype(F32) + inv * scaled - x_head * (inv * inv * inv) * mean[..., None]
-    grad = lax.all_to_all(grad.astype(BF16), "row", 0, 0)
-    grad = grad.transpose(1, 0, 2).reshape(1, tall, across, width)
-    return shift(grad, "pipe", -1)
+    gains = section_gains[0]
+    x3, r3, cot = gather(saved_in.reshape(area, width), cotangent.reshape(area, width))
+    own, left, right = attention(x3, r3, cot, gains)
+    grad = scatter(own, left, right, x3, r3, cot, gains)
+    return grad.reshape(1, tall, across, width)
 
 
 def solution(mesh):

time: 297 us -> 164 us (0.55)
  the two profiles are of different devices: /device:TPU:16 before, /device:TPU:47 now
where the time goes in v1:
time: 164 us
  Pallas kernels  160 us (98%)
  local copies, waits for them, and re-layouts  3.31 us (2%)
    pallas_call x1, Pallas kernels, gather(): pl.pallas_call(gather_kernel, out_shape=(jax.ShapeDtypeStruct((3, HEADS,...  62.7 us
    pallas_call x1, Pallas kernels, scatter(): pl.pallas_call(scatter_kernel, out_shape=jax.ShapeDtypeStruct((area, rows...  59.7 us
    pallas_call x1, Pallas kernels, attention(): pl.pallas_call(attention_kernel, out_shape=(block, block, block), in_spec...  38 us
    unnamed x2, local copies, waits for them, and re-layouts  3.31 us

profile of v1, /device:TPU:47, one launch (start us, length us, event | category | flops | bytes accessed | tf_op | source)
XLA Modules:
  0.0 163.7 jit_solution(6768440109740837183)
XLA Ops:
  0.0 1.4 copy.6
  1.4 62.7 %gather_heads.1 = (bf16[3,16,128,128]{3,2,1,0:T(8,128)(2,1)}, f32[3,16,8,128]{3,2,1,0:T(8,128)}, bf16[16,128,128]{2,1,0:T(8,128)(2,1)}) custom-call(bf16[128,2048]{1,0:T(8,128)(2,1)} %bitcast.6, bf16[128,2048]{1,0:T(8,128)(2,1)} %bitcast.7, bf16[128,2048]{1,0:T(8,128)(2,1)} %bitcast.11), custom_call_target="tpu_custom_call" | custom-call | tf_op jit(solution)/shard_map/gather_heads/pallas_call | solution.py:350
  64.1 38.0 %head_attention.1 = (f32[16,128,128]{2,1,0:T(8,128)}, f32[16,128,128]{2,1,0:T(8,128)}, f32[16,128,128]{2,1,0:T(8,128)}) custom-call(bf16[3,16,128,128]{3,2,1,0:T(8,128)(2,1)} %get-tuple-element.11.refs_0_.x3_far, f32[3,16,8,128]{3,2,1,0:T(8,128)} %get-tuple-element.12.refs_1_.r3_far, bf16[16,128,128]{2,1,0:T(8,128)(2,1)} %get-tuple-element.13.refs_2_.cot_ref, ...), custom_call_target="tpu_custom_call" | custom-call | tf_op jit(solution)/shard_map/head_attention/pallas_call | solution.py:152
  102.1 59.7 %finish_and_return.1 = bf16[128,2048]{1,0:T(8,128)(2,1)} custom-call(f32[16,128,128]{2,1,0:T(8,128)} %get-tuple-element.14.own_ref, f32[16,128,128]{2,1,0:T(8,128)} %get-tuple-element.15.left_far, f32[16,128,128]{2,1,0:T(8,128)} %get-tuple-element.16.right_far, bf16[3,16,128,128]{3,2,1,0:T(8,128)(2,1)} %get-tuple-element.11.refs_0_.x3_far, ...), custom_call_target="tpu_custom_call" | custom-call | tf_op jit(solution)/shard_map/finish_and_return/pallas_call | solution.py:565
  161.9 1.9 %copy.8 = bf16[1,8,16,2048]{3,2,1,0:T(8,128)(2,1)} copy(bf16[1,8,16,2048]{3,2,1,0:T(8,128)(2,1)} %bitcast.8) | data formatting | bytes 1048576

commit v2 on v0

v2 whole, which is shorter than its diff:
```python
import math

import jax
import jax.numpy as jnp
from jax import lax
from jax.experimental import pallas as pl
from jax.experimental.pallas import tpu as pltpu
from jax.sharding import PartitionSpec as P

HEADS = 16
HEAD_DIM = 128
TILE = 8
SPAN = 5
REACH = SPAN // 2
TERMS_LAG = 2
MEAN_LAG = 4

NEGATIVE = -1e30
EPSILON = 1e-06
F32 = jnp.float32
BF16 = jnp.bfloat16
MESH = pl.DeviceIdType.MESH


def dot(left, right, dims):
    return lax.dot_general(left, right, (dims, ((), ())), preferred_element_type=F32)


def fold(block, op):
    rows, lanes = block.shape
    return op(block.reshape(rows // 8, 8, lanes), axis=0)


def head_lanes(head):
    return pl.ds(pl.multiple_of(head * HEAD_DIM, HEAD_DIM), HEAD_DIM)


def remote(src, dst, send, recv, device):
    return pltpu.make_async_remote_copy(
        src_ref=src, dst_ref=dst, send_sem=send, recv_sem=recv,
        device_id=device, device_id_type=MESH,
    )


def loop(low, high, step):
    def body(index, carry):
        step(index)
        return carry

    lax.fori_loop(low, high, body, 0)


def section_kernel(
    x_ref, x_far, cot_far, gains_far, out_ref,
    x3_ref, r3_ref, cot_ref, gains_ref, inv_ref, bias_ref, kv_ref, kt_ref, qd_ref, w_ref,
    p_ref, dp_ref, own_ref, term_ref, from_ref, part_ref, mean_ref, grad_ref,
    local_sem, x_send, x_recv, r_send, r_recv, c_send, c_recv,
    fx_send, fx_recv, fr_send, fr_recv, t_send, t_recv, m_local, m_send, m_recv, g_send, g_recv,
):
    area = x_ref.shape[0]
    rows = HEADS
    depth = HEAD_DIM
    wide = 3 * area
    me = lax.axis_index("row")
    col = lax.axis_index("col")
    cols = lax.axis_size("col")
    pipe = lax.axis_index("pipe")
    pipes = lax.axis_size("pipe")
    has_left = col > 0
    has_right = col < cols - 1
    barrier = pltpu.get_barrier_semaphore()

    def greet(device):
        pl.semaphore_signal(barrier, inc=1, device_id=device, device_id_type=MESH)

    def to(hop):
        return lax.rem(me + hop, HEADS)

    def back(hop):
        return lax.rem(me + HEADS - hop, HEADS)

    def both(act):
        @pl.when(has_left)
        def _():
            act(0)

        @pl.when(has_right)
        def _():
            act(1)

    def side_device(side):
        return {"col": col - 1} if side == 0 else {"col": col + 1}

    def x_copy(src, dst):
        return remote(
            x_far.at[:, head_lanes(dst)], x3_ref.at[1, src], x_send.at[dst], x_recv.at[src],
            {"row": dst},
        )

    def r_copy(src, dst):
        return remote(inv_ref, r3_ref.at[1, src], r_send.at[dst], r_recv.at[src], {"row": dst})

    def c_copy(src, dst):
        return remote(
            cot_far.at[:, head_lanes(dst)], cot_ref.at[src], c_send.at[dst], c_recv.at[src],
            {"row": dst},
        )

    def fx_copy(src, side):
        return remote(
            x3_ref.at[1, src], x3_ref.at[2 - 2 * side, src], fx_send.at[side, src],
            fx_recv.at[side, src], side_device(side),
        )

    def fr_copy(src, side):
        return remote(
            r3_ref.at[1, src], r3_ref.at[2 - 2 * side, src], fr_send.at[side, src],
            fr_recv.at[side, src], side_device(side),
        )

    def t_copy(row, side):
        return remote(
            term_ref.at[side, row], from_ref.at[side, row], t_send.at[side, row],
            t_recv.at[side, row], side_device(side),
        )

    def m_copy(row, src, dst):
        return remote(
            part_ref.at[pl.ds(row, 1)], mean_ref.at[row, pl.ds(src, 1)],
            m_send.at[row, dst], m_recv.at[row, src], {"row": dst},
        )

    def g_copy(src, dst):
        return remote(
            grad_ref.at[dst], out_ref.at[:, head_lanes(src)], g_send.at[dst], g_recv.at[src],
            {"pipe": pipe - 1, "row": dst},
        )

    def work():
        loop(1, HEADS, lambda hop: greet({"row": to(hop)}))
        both(lambda side: greet(side_device(side)))
        local = [
            pltpu.make_async_copy(x_far.at[:, head_lanes(me)], x3_ref.at[1, me], local_sem.at[0]),
            pltpu.make_async_copy(cot_far.at[:, head_lanes(me)], cot_ref.at[me], local_sem.at[1]),
            pltpu.make_async_copy(gains_far.at[:, :, head_lanes(me)], gains_ref, local_sem.at[2]),
        ]
        for copy in local:
            copy.start()
        x_float = x_ref[...].astype(F32)
        square = jnp.mean(x_float * x_float, axis=-1, keepdims=True)
        inverse = jnp.broadcast_to(lax.rsqrt(square + EPSILON), (area, area))
        inv_ref[...] = inverse.T[:8]

        key = lax.broadcasted_iota(jnp.int32, (wide, area), 0)
        query = lax.broadcasted_iota(jnp.int32, (wide, area), 1)
        key_tile = 2 * (key // area) + (key // TILE) % 2
        query_tile = (query // TILE) % 2
        near = (key_tile >= query_tile) & (key_tile <= query_tile + 2 * REACH)
        inside = (col * 2 + key_tile >= REACH) & (col * 2 + key_tile < 2 * cols + REACH)
        bias_ref[0] = jnp.full((wide, area), NEGATIVE, F32)
        bias_ref[1] = jnp.where(near & inside, 0.0, NEGATIVE)
        for pad in (0, 1, rows + 2, rows + 3):
            kv_ref[pad] = jnp.zeros((wide, 2 * depth), BF16)
            kt_ref[pad] = jnp.zeros((depth, wide), BF16)
            qd_ref[pad] = jnp.zeros((2 * area, 2 * depth), BF16)
        for key_line, slot in ((0, 0), (0, 1), (1, 0), (rows - 2, 4), (rows - 1, 3), (rows - 1, 4)):
            w_ref[key_line + REACH, :, slot * 2 * area : (slot + 1) * 2 * area] = jnp.zeros(
                (wide, 2 * area), BF16
            )
        pl.semaphore_wait(
            barrier, 2 * HEADS - 1 + has_left.astype(jnp.int32) + has_right.astype(jnp.int32)
        )

        loop(1, HEADS, lambda hop: x_copy(me, to(hop)).start())
        loop(1, HEADS, lambda hop: r_copy(me, to(hop)).start())
        own_r = pltpu.make_async_copy(inv_ref, r3_ref.at[1, me], local_sem.at[3])
        own_r.start()
        loop(1, HEADS, lambda hop: c_copy(me, to(hop)).start())
        for copy in local:
            copy.wait()
        own_r.wait()

        gn = gains_ref[0]
        gq = gains_ref[1] * (1.0 / math.sqrt(HEAD_DIM))
        gk = gains_ref[2]
        gv = gains_ref[3]
        go = gains_ref[4]

        def prepare(row, block):
            inverse = jnp.broadcast_to(r3_ref[block, row, 0:1, :], (area, area)).T
            x_float = x3_ref[block, row].astype(F32)
            normed = (x_float * inverse * gn).astype(BF16).astype(F32)
            keys = (normed * gk).astype(BF16)
            lanes = slice(block * area, (block + 1) * area)
            kv_ref[row + REACH, lanes, :depth] = keys
            kv_ref[row + REACH, lanes, depth:] = (normed * gv).astype(BF16)
            kt_ref[row + REACH, :, lanes] = keys.T
            if block == 1:
                qd_ref[row + REACH, :area, :depth] = (normed * gq).astype(BF16)
                qd_ref[row + REACH, :area, depth:] = jnp.zeros((area, depth), BF16)
                qd_ref[row + REACH, area:, :depth] = jnp.zeros((area, depth), BF16)

        def pass_on(src):
            both(lambda side: fx_copy(src, side).start())
            both(lambda side: fr_copy(src, side).start())
            prepare(src, 1)

        pass_on(me)

        def arrive(hop):
            src = back(hop)
            x_copy(src, me).wait_recv()
            r_copy(src, me).wait_recv()
            pass_on(src)

        loop(1, HEADS, arrive)

        def beside(hop):
            src = back(hop)
            for block, side in ((2, 0), (0, 1)):
                present = has_left if block == 0 else has_right
                lanes = slice(block * area, (block + 1) * area)

                @pl.when(present)
                def _():
                    fx_copy(src, side).wait_recv()
                    fr_copy(src, side).wait_recv()
                    prepare(src, block)

                @pl.when(jnp.logical_not(present))
                def _():
                    kv_ref[src + REACH, lanes, :] = jnp.zeros((area, 2 * depth), BF16)
                    kt_ref[src + REACH, :, lanes] = jnp.zeros((depth, area), BF16)

        loop(0, HEADS, beside)

        def soften(row):
            queries = qd_ref[row + REACH, :area, :depth]
            top = jnp.full((8, area), NEGATIVE, F32)
            for off in range(SPAN):
                far = row + off - REACH
                valid = jnp.logical_and(far >= 0, far < rows).astype(jnp.int32)
                scores = dot(kv_ref[row + off, :, :depth], queries, ((1,), (1,))) + bias_ref[valid]
                p_ref[row, off] = scores
                top = jnp.maximum(top, fold(scores, jnp.max))
            top = jnp.max(top, axis=0, keepdims=True)
            total = jnp.zeros((8, area), F32)
            for off in range(SPAN):
                raised = jnp.exp(p_ref[row, off] - top)
                p_ref[row, off] = raised
                total = total + fold(raised, jnp.sum)
            scale = 1.0 / jnp.sum(total, axis=0, keepdims=True)
            for off in range(SPAN):
                weights = p_ref[row, off] * scale
                p_ref[row, off] = weights
                slot = SPAN - 1 - off
                w_ref[row + off, :, slot * 2 * area + area : (slot + 1) * 2 * area] = weights.astype(
                    BF16
                )

        loop(0, rows, soften)

        def upstream(hop):
            src = back(hop)

            @pl.when(hop > 0)
            def _():
                c_copy(src, me).wait_recv()

            qd_ref[src + REACH, area:, depth:] = (cot_ref[src].astype(F32) * go).astype(BF16)

        loop(0, HEADS, upstream)

        def grade(row):
            grads = qd_ref[row + REACH, area:, depth:]
            delta = jnp.zeros((8, area), F32)
            for off in range(SPAN):
                slot = SPAN - 1 - off
                product = dot(kv_ref[row + off, :, depth:], grads, ((1,), (1,)))
                dp_ref[off] = product
                rounded = w_ref[row + off, :, slot * 2 * area + area : (slot + 1) * 2 * area]
                delta = delta + fold(rounded.astype(F32) * product, jnp.sum)
            delta = jnp.sum(delta, axis=0, keepdims=True)
            turned = jnp.zeros((depth, area), F32)
            for off in range(SPAN):
                slot = SPAN - 1 - off
                dscore = (p_ref[row, off] * (dp_ref[off] - delta)).astype(BF16)
                w_ref[row + off, :, slot * 2 * area : slot * 2 * area + area] = dscore
                turned = turned + dot(kt_ref[row + off], dscore, ((1,), (0,)))
            own_ref[row] = turned.T * gq

        def key_line(row):
            pairs = qd_ref[pl.ds(row, SPAN)].reshape(SPAN * 2 * area, 2 * depth)
            grads = dot(w_ref[row + REACH], pairs, ((1,), (0,)))
            terms = grads[:, :depth] * gk + grads[:, depth:] * gv
            term_ref[0, row] = terms[:area]
            own_ref[row] = own_ref[row] + terms[area : 2 * area]
            term_ref[1, row] = terms[2 * area :]

        def collect(row):
            both(lambda side: t_copy(row, 1 - side).wait_recv())
            dnormed = own_ref[row]
            dnormed = dnormed + jnp.where(has_right, from_ref[0, row], 0.0)
            dnormed = dnormed + jnp.where(has_left, from_ref[1, row], 0.0)
            scaled = dnormed * gn
            own_ref[row] = scaled
            product = (x3_ref[1, row].astype(F32) * scaled).T
            part_ref[pl.ds(row, 1), :] = jnp.sum(product, axis=0, keepdims=True)

        def own_part(row):
            return pltpu.make_async_copy(
                part_ref.at[pl.ds(row, 1)], mean_ref.at[row, pl.ds(me, 1)], m_local.at[row]
            )

        def share(row):
            own_part(row).start()
            loop(1, HEADS, lambda hop: m_copy(row, me, to(hop)).start())

        def close(row):
            own_part(row).wait()
            loop(1, HEADS, lambda hop: m_copy(row, back(hop), me).wait_recv())
            mean = jnp.sum(mean_ref[row], axis=0, keepdims=True) / (rows * depth)
            inverse = jnp.broadcast_to(r3_ref[1, row, 0:1, :], (area, area))
            pull = (inverse * inverse * inverse * mean).T
            grad = (
                cot_ref[row].astype(F32)
                + inverse.T * own_ref[row]
                - x3_ref[1, row].astype(F32) * pull
            )
            grad_ref[row] = grad.astype(BF16)

        stages = (
            (grade, 0),
            (key_line, REACH),
            (lambda row: both(lambda side: t_copy(row, side).start()), REACH + 1),
            (collect, REACH + 1 + TERMS_LAG),
            (share, REACH + 2 + TERMS_LAG),
            (close, REACH + 2 + TERMS_LAG + MEAN_LAG),
            (lambda row: g_copy(me, row).start(), REACH + 3 + TERMS_LAG + MEAN_LAG),
        )

        def advance(step):
            for act, lag in stages:
                @pl.when(jnp.logical_and(step >= lag, step < rows + lag))
                def _():
                    act(step - lag)

        loop(0, rows + stages[-1][1], advance)

    @pl.when(pipe < pipes - 1)
    def _():
        loop(0, rows, lambda row: greet({"pipe": pipe + 1, "row": row}))

    @pl.when(pipe == pipes - 1)
    def _():
        out_ref[...] = jnp.zeros_like(out_ref)

    @pl.when(pipe > 0)
    def _():
        work()

    @pl.when(pipe < pipes - 1)
    def _():
        def wait_grad(row):
            remote(
                grad_ref.at[0], out_ref.at[:, head_lanes(row)], g_send.at[0], g_recv.at[row],
                {"pipe": pipe + 1, "row": row},
            ).wait_recv()

        loop(0, rows, wait_grad)

    @pl.when(pipe > 0)
    def _():
        def drain(hop):
            x_copy(me, to(hop)).wait_send()
            r_copy(me, to(hop)).wait_send()
            c_copy(me, to(hop)).wait_send()

        loop(1, HEADS, drain)

        def drain_row(row):
            both(lambda side: fx_copy(row, side).wait_send())
            both(lambda side: fr_copy(row, side).wait_send())
            both(lambda side: t_copy(row, side).wait_send())
            loop(1, HEADS, lambda hop: m_copy(row, me, to(hop)).wait_send())
            g_copy(me, row).wait_send()

        loop(0, rows, drain_row)


def per_device(saved_in, cotangent, section_gains):
    _, tall, across, width = saved_in.shape
    area = tall * across
    rows = HEADS
    wide = 3 * area
    x = saved_in.reshape(area, width)
    cot = cotangent.reshape(area, width)
    gains = section_gains.transpose(1, 0, 2)
    far = pl.BlockSpec(memory_space=pl.ANY)
    vmem = pl.BlockSpec(memory_space=pltpu.VMEM)
    dma = pltpu.SemaphoreType.DMA
    grad = pl.pallas_call(
        section_kernel,
        out_shape=jax.ShapeDtypeStruct((area, width), BF16),
        in_specs=[vmem, far, far, far],
        out_specs=vmem,
        scratch_shapes=[
            pltpu.VMEM((3, rows, area, HEAD_DIM), BF16),
            pltpu.VMEM((3, rows, 8, area), F32),
            pltpu.VMEM((rows, area, HEAD_DIM), BF16),
            pltpu.VMEM((gains.shape[0], 1, HEAD_DIM), F32),
            pltpu.VMEM((8, area), F32),
            pltpu.VMEM((2, wide, area), F32),
            pltpu.VMEM((rows + 4, wide, 2 * HEAD_DIM), BF16),
            pltpu.VMEM((rows + 4, HEAD_DIM, wide), BF16),
            pltpu.VMEM((rows + 4, 2 * area, 2 * HEAD_DIM), BF16),
            pltpu.VMEM((rows + 4, wide, SPAN * 2 * area), BF16),
            pltpu.VMEM((rows, SPAN, wide, area), F32),
            pltpu.VMEM((SPAN, wide, area), F32),
            pltpu.VMEM((rows, area, HEAD_DIM), F32),
            pltpu.VMEM((2, rows, area, HEAD_DIM), F32),
            pltpu.VMEM((2, rows, area, HEAD_DIM), F32),
            pltpu.VMEM((rows, area), F32),
            pltpu.VMEM((rows, HEADS, area), F32),
            pltpu.VMEM((rows, area, HEAD_DIM), BF16),
            dma((4,)),
            dma((HEADS,)), dma((HEADS,)), dma((HEADS,)), dma((HEADS,)), dma((HEADS,)), dma((HEADS,)),
            dma((2, HEADS)), dma((2, HEADS)), dma((2, HEADS)), dma((2, HEADS)),
            dma((2, rows)), dma((2, rows)),
            dma((rows,)), dma((rows, HEADS)), dma((rows, HEADS)),
            dma((rows,)), dma((HEADS,)),
        ],
        compiler_params=pltpu.CompilerParams(
            collective_id=0, has_side_effects=True, vmem_limit_bytes=60 * 1024 * 1024
        ),
        name="section_backward",
    )(x, x, cot, gains)
    return grad.reshape(1, tall, across, width)


def solution(mesh):
    return jax.shard_map(
        per_device,
        mesh=mesh,
        in_specs=(
            P("pipe", "row", "col", None),
            P("pipe", "row", "col", None),
            P("pipe", None, None),
        ),
        out_specs=P("pipe", "row", "col", None),
        check_vma=False,
    )
```

time: 297 us -> 135 us (0.45)
  the two profiles are of different devices: /device:TPU:16 before, /device:TPU:6 now
where the time goes in v2:
time: 135 us
  Pallas kernels  133 us (99%)
  local copies, waits for them, and re-layouts  1.88 us (1%)
    pallas_call x1, Pallas kernels, per_device(): pl.pallas_call(section_kernel, out_shape=jax.ShapeDtypeStruct((area, widt...  133 us

profile of v2, /device:TPU:6, one launch (start us, length us, event | category | flops | bytes accessed | tf_op | source)
XLA Modules:
  0.0 135.0 jit_solution(10409378266903032269)
XLA Ops:
  0.0 133.1 %section_backward.1 = bf16[128,2048]{1,0:T(8,128)(2,1)} custom-call(bf16[128,2048]{1,0:T(8,128)(2,1)} %bitcast.5, bf16[128,2048]{1,0:T(8,128)(2,1)} %bitcast.6, bf16[128,2048]{1,0:T(8,128)(2,1)} %bitcast.7, f32[5,1,2048]{2,1,0:T(1,128)} %bitcast.8), custom_call_target="tpu_custom_call" | custom-call | tf_op jit(solution)/shard_map/section_backward/pallas_call | solution.py:402
  133.1 1.9 %copy.5 = bf16[1,8,16,2048]{3,2,1,0:T(8,128)(2,1)} copy(bf16[1,8,16,2048]{3,2,1,0:T(8,128)(2,1)} %bitcast.4) | data formatting | bytes 1048576

commit v3 on v2

--- a/solution.py
+++ b/solution.py
@@ -1,3 +1,4 @@
+import functools
 import math
 
 import jax
@@ -12,8 +13,9 @@
 TILE = 8
 SPAN = 5
 REACH = SPAN // 2
-TERMS_LAG = 2
-MEAN_LAG = 4
+GROUP = 4
+TERMS_LAG = 1
+MEAN_LAG = 7
 
 NEGATIVE = -1e30
 EPSILON = 1e-06
@@ -53,7 +55,7 @@
 def section_kernel(
     x_ref, x_far, cot_far, gains_far, out_ref,
     x3_ref, r3_ref, cot_ref, gains_ref, inv_ref, bias_ref, kv_ref, kt_ref, qd_ref, w_ref,
-    p_ref, dp_ref, own_ref, term_ref, from_ref, part_ref, mean_ref, grad_ref,
+    p_ref, scale_ref, dp_ref, own_ref, term_ref, from_ref, part_ref, mean_ref, grad_ref,
     local_sem, x_send, x_recv, r_send, r_recv, c_send, c_recv,
     fx_send, fx_recv, fr_send, fr_recv, t_send, t_recv, m_local, m_send, m_recv, g_send, g_recv,
 ):
@@ -124,10 +126,10 @@
             t_recv.at[side, row], side_device(side),
         )
 
-    def m_copy(row, src, dst):
-        return remote(
-            part_ref.at[pl.ds(row, 1)], mean_ref.at[row, pl.ds(src, 1)],
-            m_send.at[row, dst], m_recv.at[row, src], {"row": dst},
+    def m_copy(group, src, dst):
+        return remote(
+            part_ref.at[group], mean_ref.at[group, src],
+            m_send.at[group, dst], m_recv.at[group, src], {"row": dst},
         )
 
     def g_copy(src, dst):
@@ -149,7 +151,7 @@
         x_float = x_ref[...].astype(F32)
         square = jnp.mean(x_float * x_float, axis=-1, keepdims=True)
         inverse = jnp.broadcast_to(lax.rsqrt(square + EPSILON), (area, area))
-        inv_ref[...] = inverse.T[:8]
+        inv_ref[...] = inverse.T[:1]
 
         key = lax.broadcasted_iota(jnp.int32, (wide, area), 0)
         query = lax.broadcasted_iota(jnp.int32, (wide, area), 1)
@@ -171,8 +173,8 @@
             barrier, 2 * HEADS - 1 + has_left.astype(jnp.int32) + has_right.astype(jnp.int32)
         )
 
+        loop(1, HEADS, lambda hop: r_copy(me, to(hop)).start())
         loop(1, HEADS, lambda hop: x_copy(me, to(hop)).start())
-        loop(1, HEADS, lambda hop: r_copy(me, to(hop)).start())
         own_r = pltpu.make_async_copy(inv_ref, r3_ref.at[1, me], local_sem.at[3])
         own_r.start()
         loop(1, HEADS, lambda hop: c_copy(me, to(hop)).start())
@@ -187,7 +189,7 @@
         go = gains_ref[4]
 
         def prepare(row, block):
-            inverse = jnp.broadcast_to(r3_ref[block, row, 0:1, :], (area, area)).T
+            inverse = jnp.broadcast_to(r3_ref[block, row], (area, area)).T
             x_float = x3_ref[block, row].astype(F32)
             normed = (x_float * inverse * gn).astype(BF16).astype(F32)
             keys = (normed * gk).astype(BF16)
@@ -215,48 +217,74 @@
 
         loop(1, HEADS, arrive)
 
-        def beside(hop):
-            src = back(hop)
-            for block, side in ((2, 0), (0, 1)):
-                present = has_left if block == 0 else has_right
-                lanes = slice(block * area, (block + 1) * area)
-
-                @pl.when(present)
-                def _():
-                    fx_copy(src, side).wait_recv()
-                    fr_copy(src, side).wait_recv()
-                    prepare(src, block)
-
-                @pl.when(jnp.logical_not(present))
-                def _():
-                    kv_ref[src + REACH, lanes, :] = jnp.zeros((area, 2 * depth), BF16)
-                    kt_ref[src + REACH, :, lanes] = jnp.zeros((depth, area), BF16)
-
-        loop(0, HEADS, beside)
+        def await_beside(src, side):
+            fx_copy(src, side).wait_recv()
+            fr_copy(src, side).wait_recv()
+
+        def blank(src, block):
+            lanes = slice(block * area, (block + 1) * area)
+            kv_ref[src + REACH, lanes, :] = jnp.zeros((area, 2 * depth), BF16)
+            kt_ref[src + REACH, :, lanes] = jnp.zeros((depth, area), BF16)
+
+        def beside(pair):
+            sources = (back(2 * pair), back(2 * pair + 1))
+
+            @pl.when(jnp.logical_and(has_left, has_right))
+            def _():
+                for src in sources:
+                    await_beside(src, 0)
+                    await_beside(src, 1)
+                for src in sources:
+                    prepare(src, 0)
+                    prepare(src, 2)
+
+            @pl.when(jnp.logical_not(has_left))
+            def _():
+                for src in sources:
+                    await_beside(src, 0)
+                for src in sources:
+                    prepare(src, 2)
+                    blank(src, 0)
+
+            @pl.when(jnp.logical_not(has_right))
+            def _():
+                for src in sources:
+                    await_beside(src, 1)
+                for src in sources:
+                    prepare(src, 0)
+                    blank(src, 2)
+
+        loop(0, HEADS // 2, beside)
+
+        def lines_of(block):
+            return slice(block * area, (block + 1) * area)
 
         def soften(row):
             queries = qd_ref[row + REACH, :area, :depth]
-            top = jnp.full((8, area), NEGATIVE, F32)
+            tops = []
+            totals = []
             for off in range(SPAN):
                 far = row + off - REACH
-                valid = jnp.logical_and(far >= 0, far < rows).astype(jnp.int32)
-                scores = dot(kv_ref[row + off, :, :depth], queries, ((1,), (1,))) + bias_ref[valid]
-                p_ref[row, off] = scores
-                top = jnp.maximum(top, fold(scores, jnp.max))
-            top = jnp.max(top, axis=0, keepdims=True)
-            total = jnp.zeros((8, area), F32)
-            for off in range(SPAN):
-                raised = jnp.exp(p_ref[row, off] - top)
-                p_ref[row, off] = raised
-                total = total + fold(raised, jnp.sum)
-            scale = 1.0 / jnp.sum(total, axis=0, keepdims=True)
-            for off in range(SPAN):
-                weights = p_ref[row, off] * scale
-                p_ref[row, off] = weights
-                slot = SPAN - 1 - off
-                w_ref[row + off, :, slot * 2 * area + area : (slot + 1) * 2 * area] = weights.astype(
-                    BF16
-                )
+                valid = jnp.logical_and(far >= 0, far < rows)
+                index = valid.astype(jnp.int32)
+                for block in range(3):
+                    lines = lines_of(block)
+                    scores = dot(kv_ref[row + off, lines, :depth], queries, ((1,), (1,)))
+                    if block == 1:
+                        scores = scores + jnp.where(valid, 0.0, NEGATIVE)
+                    else:
+                        scores = scores + bias_ref[index, lines, :]
+                    top = jnp.max(fold(scores, jnp.max), axis=0, keepdims=True)
+                    raised = jnp.exp(scores - top)
+                    p_ref[row, off, lines, :] = raised
+                    tops.append(top)
+                    totals.append(fold(raised, jnp.sum))
+            peak = functools.reduce(jnp.maximum, tops)
+            shares = [jnp.exp(top - peak) for top in tops]
+            total = jnp.sum(sum(t * f for t, f in zip(totals, shares)), axis=0, keepdims=True)
+            inverse = 1.0 / total
+            for index, share in enumerate(shares):
+                scale_ref[row, index : index + 1, :] = share * inverse
 
         loop(0, rows, soften)
 
@@ -275,17 +303,29 @@
             grads = qd_ref[row + REACH, area:, depth:]
             delta = jnp.zeros((8, area), F32)
             for off in range(SPAN):
-                slot = SPAN - 1 - off
-                product = dot(kv_ref[row + off, :, depth:], grads, ((1,), (1,)))
-                dp_ref[off] = product
-                rounded = w_ref[row + off, :, slot * 2 * area + area : (slot + 1) * 2 * area]
-                delta = delta + fold(rounded.astype(F32) * product, jnp.sum)
+                slot = 2 * area * (SPAN - 1 - off)
+                for block in range(3):
+                    lines = lines_of(block)
+                    index = 3 * off + block
+                    product = dot(kv_ref[row + off, lines, depth:], grads, ((1,), (1,)))
+                    dp_ref[off, lines, :] = product
+                    weights = p_ref[row, off, lines, :] * scale_ref[row, index : index + 1, :]
+                    rounded = weights.astype(BF16)
+                    w_ref[row + off, lines, slot + area : slot + 2 * area] = rounded
+                    delta = delta + fold(rounded.astype(F32) * product, jnp.sum)
             delta = jnp.sum(delta, axis=0, keepdims=True)
             turned = jnp.zeros((depth, area), F32)
             for off in range(SPAN):
-                slot = SPAN - 1 - off
-                dscore = (p_ref[row, off] * (dp_ref[off] - delta)).astype(BF16)
-                w_ref[row + off, :, slot * 2 * area : slot * 2 * area + area] = dscore
+                slot = 2 * area * (SPAN - 1 - off)
+                pieces = []
+                for block in range(3):
+                    lines = lines_of(block)
+                    index = 3 * off + block
+                    weights = p_ref[row, off, lines, :] * scale_ref[row, index : index + 1, :]
+                    dscore = (weights * (dp_ref[off, lines, :] - delta)).astype(BF16)
+                    w_ref[row + off, lines, slot : slot + area] = dscore
+                    pieces.append(dscore)
+                dscore = jnp.concatenate(pieces, axis=0)
                 turned = turned + dot(kt_ref[row + off], dscore, ((1,), (0,)))
             own_ref[row] = turned.T * gq
 
@@ -305,29 +345,45 @@
             scaled = dnormed * gn
             own_ref[row] = scaled
             product = (x3_ref[1, row].astype(F32) * scaled).T
-            part_ref[pl.ds(row, 1), :] = jnp.sum(product, axis=0, keepdims=True)
-
-        def own_part(row):
+            part_ref[row // GROUP, pl.ds(row % GROUP, 1), :] = jnp.sum(
+                product, axis=0, keepdims=True
+            )
+
+        def own_part(group):
             return pltpu.make_async_copy(
-                part_ref.at[pl.ds(row, 1)], mean_ref.at[row, pl.ds(me, 1)], m_local.at[row]
+                part_ref.at[group], mean_ref.at[group, me], m_local.at[group]
             )
 
         def share(row):
-            own_part(row).start()
-            loop(1, HEADS, lambda hop: m_copy(row, me, to(hop)).start())
+            @pl.when(row % GROUP == GROUP - 1)
+            def _():
+                group = row // GROUP
+                own_part(group).start()
+                loop(1, HEADS, lambda hop: m_copy(group, me, to(hop)).start())
 
         def close(row):
-            own_part(row).wait()
-            loop(1, HEADS, lambda hop: m_copy(row, back(hop), me).wait_recv())
-            mean = jnp.sum(mean_ref[row], axis=0, keepdims=True) / (rows * depth)
-            inverse = jnp.broadcast_to(r3_ref[1, row, 0:1, :], (area, area))
-            pull = (inverse * inverse * inverse * mean).T
-            grad = (
-                cot_ref[row].astype(F32)
-                + inverse.T * own_ref[row]
-                - x3_ref[1, row].astype(F32) * pull
-            )
-            grad_ref[row] = grad.astype(BF16)
+            @pl.when(row % GROUP == GROUP - 1)
+            def _():
+                group = row // GROUP
+                own_part(group).wait()
+                loop(1, HEADS, lambda hop: m_copy(group, back(hop), me).wait_recv())
+                means = jnp.sum(mean_ref[group], axis=0) / (rows * depth)
+                for line in range(GROUP):
+                    each = group * GROUP + line
+                    inverse = jnp.broadcast_to(r3_ref[1, each], (area, area))
+                    pull = (inverse * inverse * inverse * means[line : line + 1]).T
+                    grad = (
+                        cot_ref[each].astype(F32)
+                        + inverse.T * own_ref[each]
+                        - x3_ref[1, each].astype(F32) * pull
+                    )
+                    grad_ref[each] = grad.astype(BF16)
+
+        def give_back(row):
+            @pl.when(row % GROUP == GROUP - 1)
+            def _():
+                for line in range(GROUP):
+                    g_copy(me, row - line).start()
 
         stages = (
             (grade, 0),
@@ -336,7 +392,7 @@
             (collect, REACH + 1 + TERMS_LAG),
             (share, REACH + 2 + TERMS_LAG),
             (close, REACH + 2 + TERMS_LAG + MEAN_LAG),
-            (lambda row: g_copy(me, row).start(), REACH + 3 + TERMS_LAG + MEAN_LAG),
+            (give_back, REACH + 3 + TERMS_LAG + MEAN_LAG),
         )
 
         def advance(step):
@@ -382,10 +438,14 @@
             both(lambda side: fx_copy(row, side).wait_send())
             both(lambda side: fr_copy(row, side).wait_send())
             both(lambda side: t_copy(row, side).wait_send())
-            loop(1, HEADS, lambda hop: m_copy(row, me, to(hop)).wait_send())
             g_copy(me, row).wait_send()
 
         loop(0, rows, drain_row)
+
+        def drain_group(group):
+            loop(1, HEADS, lambda hop: m_copy(group, me, to(hop)).wait_send())
+
+        loop(0, rows // GROUP, drain_group)
 
 
 def per_device(saved_in, cotangent, section_gains):
@@ -406,28 +466,29 @@
         out_specs=vmem,
         scratch_shapes=[
             pltpu.VMEM((3, rows, area, HEAD_DIM), BF16),
-            pltpu.VMEM((3, rows, 8, area), F32),
+            pltpu.VMEM((3, rows, 1, area), F32),
             pltpu.VMEM((rows, area, HEAD_DIM), BF16),
             pltpu.VMEM((gains.shape[0], 1, HEAD_DIM), F32),
-            pltpu.VMEM((8, area), F32),
+            pltpu.VMEM((1, area), F32),
             pltpu.VMEM((2, wide, area), F32),
             pltpu.VMEM((rows + 4, wide, 2 * HEAD_DIM), BF16),
             pltpu.VMEM((rows + 4, HEAD_DIM, wide), BF16),
             pltpu.VMEM((rows + 4, 2 * area, 2 * HEAD_DIM), BF16),
             pltpu.VMEM((rows + 4, wide, SPAN * 2 * area), BF16),
             pltpu.VMEM((rows, SPAN, wide, area), F32),
+            pltpu.VMEM((rows, 3 * SPAN, area), F32),
             pltpu.VMEM((SPAN, wide, area), F32),
             pltpu.VMEM((rows, area, HEAD_DIM), F32),
             pltpu.VMEM((2, rows, area, HEAD_DIM), F32),
             pltpu.VMEM((2, rows, area, HEAD_DIM), F32),
-            pltpu.VMEM((rows, area), F32),
-            pltpu.VMEM((rows, HEADS, area), F32),
+            pltpu.VMEM((rows // GROUP, GROUP, area), F32),
+            pltpu.VMEM((rows // GROUP, HEADS, GROUP, area), F32),
             pltpu.VMEM((rows, area, HEAD_DIM), BF16),
             dma((4,)),
             dma((HEADS,)), dma((HEADS,)), dma((HEADS,)), dma((HEADS,)), dma((HEADS,)), dma((HEADS,)),
             dma((2, HEADS)), dma((2, HEADS)), dma((2, HEADS)), dma((2, HEADS)),
             dma((2, rows)), dma((2, rows)),
-            dma((rows,)), dma((rows, HEADS)), dma((rows, HEADS)),
+            dma((rows // GROUP,)), dma((rows // GROUP, HEADS)), dma((rows // GROUP, HEADS)),
             dma((rows,)), dma((HEADS,)),
         ],
         compiler_params=pltpu.CompilerParams(

time: 135 us -> 132 us (0.978)
  the two profiles are of different devices: /device:TPU:6 before, /device:TPU:22 now
where the time goes in v3:
time: 132 us
  Pallas kernels  130 us (98%)
  local copies, waits for them, and re-layouts  1.88 us (1%)
    pallas_call x1, Pallas kernels, per_device(): pl.pallas_call(section_kernel, out_shape=jax.ShapeDtypeStruct((area, widt...  130 us

profile of v3, /device:TPU:22, one launch (start us, length us, event | category | flops | bytes accessed | tf_op | source)
XLA Modules:
  0.0 131.7 jit_solution(14104284662512382550)
XLA Ops:
  0.0 129.8 %section_backward.1 = bf16[128,2048]{1,0:T(8,128)(2,1)} custom-call(bf16[128,2048]{1,0:T(8,128)(2,1)} %bitcast.5, bf16[128,2048]{1,0:T(8,128)(2,1)} %bitcast.6, bf16[128,2048]{1,0:T(8,128)(2,1)} %bitcast.7, f32[5,1,2048]{2,1,0:T(1,128)} %bitcast.8), custom_call_target="tpu_custom_call" | custom-call | tf_op jit(solution)/shard_map/section_backward/pallas_call | solution.py:462
  129.8 1.9 %copy.5 = bf16[1,8,16,2048]{3,2,1,0:T(8,128)(2,1)} copy(bf16[1,8,16,2048]{3,2,1,0:T(8,128)(2,1)} %bitcast.4) | data formatting | bytes 1048576

commit v4 on v3

--- a/solution.py
+++ b/solution.py
@@ -15,7 +15,7 @@
 REACH = SPAN // 2
 GROUP = 4
 TERMS_LAG = 1
-MEAN_LAG = 7
+MEAN_LAG = 6
 
 NEGATIVE = -1e30
 EPSILON = 1e-06
@@ -55,7 +55,7 @@
 def section_kernel(
     x_ref, x_far, cot_far, gains_far, out_ref,
     x3_ref, r3_ref, cot_ref, gains_ref, inv_ref, bias_ref, kv_ref, kt_ref, qd_ref, w_ref,
-    p_ref, scale_ref, dp_ref, own_ref, term_ref, from_ref, part_ref, mean_ref, grad_ref,
+    p_ref, scale_ref, delta_ref, dp_ref, own_ref, term_ref, from_ref, part_ref, mean_ref, grad_ref,
     local_sem, x_send, x_recv, r_send, r_recv, c_send, c_recv,
     fx_send, fx_recv, fr_send, fr_recv, t_send, t_recv, m_local, m_send, m_recv, g_send, g_recv,
 ):
@@ -299,7 +299,7 @@
 
         loop(0, HEADS, upstream)
 
-        def grade(row):
+        def grade(row, buffer):
             grads = qd_ref[row + REACH, area:, depth:]
             delta = jnp.zeros((8, area), F32)
             for off in range(SPAN):
@@ -308,12 +308,15 @@
                     lines = lines_of(block)
                     index = 3 * off + block
                     product = dot(kv_ref[row + off, lines, depth:], grads, ((1,), (1,)))
-                    dp_ref[off, lines, :] = product
+                    dp_ref[buffer, off, lines, :] = product
                     weights = p_ref[row, off, lines, :] * scale_ref[row, index : index + 1, :]
                     rounded = weights.astype(BF16)
                     w_ref[row + off, lines, slot + area : slot + 2 * area] = rounded
                     delta = delta + fold(rounded.astype(F32) * product, jnp.sum)
-            delta = jnp.sum(delta, axis=0, keepdims=True)
+            delta_ref[row] = jnp.sum(delta, axis=0, keepdims=True)
+
+        def score(row, buffer):
+            delta = delta_ref[row]
             turned = jnp.zeros((depth, area), F32)
             for off in range(SPAN):
                 slot = 2 * area * (SPAN - 1 - off)
@@ -322,7 +325,7 @@
                     lines = lines_of(block)
                     index = 3 * off + block
                     weights = p_ref[row, off, lines, :] * scale_ref[row, index : index + 1, :]
-                    dscore = (weights * (dp_ref[off, lines, :] - delta)).astype(BF16)
+                    dscore = (weights * (dp_ref[buffer, off, lines, :] - delta)).astype(BF16)
                     w_ref[row + off, lines, slot : slot + area] = dscore
                     pieces.append(dscore)
                 dscore = jnp.concatenate(pieces, axis=0)
@@ -385,23 +388,61 @@
                 for line in range(GROUP):
                     g_copy(me, row - line).start()
 
-        stages = (
-            (grade, 0),
-            (key_line, REACH),
-            (lambda row: both(lambda side: t_copy(row, side).start()), REACH + 1),
-            (collect, REACH + 1 + TERMS_LAG),
-            (share, REACH + 2 + TERMS_LAG),
-            (close, REACH + 2 + TERMS_LAG + MEAN_LAG),
-            (give_back, REACH + 3 + TERMS_LAG + MEAN_LAG),
-        )
-
-        def advance(step):
-            for act, lag in stages:
-                @pl.when(jnp.logical_and(step >= lag, step < rows + lag))
+        def send_terms(row):
+            both(lambda side: t_copy(row, side).start())
+
+        def pair(turn):
+            first = 2 * turn
+
+            @pl.when(jnp.logical_and(turn >= 3, first < rows))
+            def _():
+                key_line(first - 5)
+                key_line(first - 4)
+                score(first - 1, 1)
+                grade(first, 0)
+                score(first, 0)
+                grade(first + 1, 1)
+
+            @pl.when(turn < 3)
+            def _():
+                @pl.when(turn == 2)
                 def _():
-                    act(step - lag)
-
-        loop(0, rows + stages[-1][1], advance)
+                    key_line(first - 4)
+
+                @pl.when(turn > 0)
+                def _():
+                    score(first - 1, 1)
+
+                grade(first, 0)
+                score(first, 0)
+                grade(first + 1, 1)
+
+            @pl.when(first == rows)
+            def _():
+                key_line(first - 5)
+                key_line(first - 4)
+                score(first - 1, 1)
+
+            @pl.when(first == rows + 2)
+            def _():
+                for line in (-5, -4, -3):
+                    key_line(first + line)
+
+            for part in range(2):
+                for act, lag in (
+                    (send_terms, 6),
+                    (collect, 6 + TERMS_LAG),
+                    (share, 7 + TERMS_LAG),
+                    (close, 7 + TERMS_LAG + MEAN_LAG),
+                    (give_back, 8 + TERMS_LAG + MEAN_LAG),
+                ):
+                    row = first + part - lag
+
+                    @pl.when(jnp.logical_and(row >= 0, row < rows))
+                    def _():
+                        act(row)
+
+        loop(0, (rows + 8 + TERMS_LAG + MEAN_LAG + 1) // 2, pair)
 
     @pl.when(pipe < pipes - 1)
     def _():
@@ -477,7 +518,8 @@
             pltpu.VMEM((rows + 4, wide, SPAN * 2 * area), BF16),
             pltpu.VMEM((rows, SPAN, wide, area), F32),
             pltpu.VMEM((rows, 3 * SPAN, area), F32),
-            pltpu.VMEM((SPAN, wide, area), F32),
+            pltpu.VMEM((rows, 1, area), F32),
+            pltpu.VMEM((2, SPAN, wide, area), F32),
             pltpu.VMEM((rows, area, HEAD_DIM), F32),
             pltpu.VMEM((2, rows, area, HEAD_DIM), F32),
             pltpu.VMEM((2, rows, area, HEAD_DIM), F32),

time: 132 us -> 135 us (1.023)
  Pallas kernels: 130 us -> 133 us
    pallas_call x1, Pallas kernels: 130 us -> 133 us  [per_device(): pl.pallas_call(section_kernel, out_shape=jax.ShapeDtypeStruct((area, widt...]
where the time goes in v4:
time: 135 us
  Pallas kernels  133 us (99%)
  local copies, waits for them, and re-layouts  1.88 us (1%)
    pallas_call x1, Pallas kernels, per_device(): pl.pallas_call(section_kernel, out_shape=jax.ShapeDtypeStruct((area, widt...  133 us

profile of v4, /device:TPU:22, one launch (start us, length us, event | category | flops | bytes accessed | tf_op | source)
XLA Modules:
  0.0 134.5 jit_solution(1726864881694427815)
XLA Ops:
  0.0 132.6 %section_backward.1 = bf16[128,2048]{1,0:T(8,128)(2,1)} custom-call(bf16[128,2048]{1,0:T(8,128)(2,1)} %bitcast.5, bf16[128,2048]{1,0:T(8,128)(2,1)} %bitcast.6, bf16[128,2048]{1,0:T(8,128)(2,1)} %bitcast.7, f32[5,1,2048]{2,1,0:T(1,128)} %bitcast.8), custom_call_target="tpu_custom_call" | custom-call | tf_op jit(solution)/shard_map/section_backward/pallas_call | solution.py:503
  132.7 1.9 %copy.5 = bf16[1,8,16,2048]{3,2,1,0:T(8,128)(2,1)} copy(bf16[1,8,16,2048]{3,2,1,0:T(8,128)(2,1)} %bitcast.4) | data formatting | bytes 1048576

commit v5 on v4

--- a/solution.py
+++ b/solution.py
@@ -14,8 +14,8 @@
 SPAN = 5
 REACH = SPAN // 2
 GROUP = 4
-TERMS_LAG = 1
-MEAN_LAG = 6
+TERMS_LAG = 4
+MEAN_LAG = 12
 
 NEGATIVE = -1e30
 EPSILON = 1e-06

time: 135 us -> 119 us (0.88)
  Pallas kernels: 133 us -> 117 us
    pallas_call x1, Pallas kernels: 133 us -> 117 us  [per_device(): pl.pallas_call(section_kernel, out_shape=jax.ShapeDtypeStruct((area, widt...]
where the time goes in v5:
time: 119 us
  Pallas kernels  117 us (98%)
  local copies, waits for them, and re-layouts  1.88 us (2%)
    pallas_call x1, Pallas kernels, per_device(): pl.pallas_call(section_kernel, out_shape=jax.ShapeDtypeStruct((area, widt...  117 us

profile of v5, /device:TPU:22, one launch (start us, length us, event | category | flops | bytes accessed | tf_op | source)
XLA Modules:
  0.0 118.6 jit_solution(4039159198277512287)
XLA Ops:
  0.0 116.7 %section_backward.1 = bf16[128,2048]{1,0:T(8,128)(2,1)} custom-call(bf16[128,2048]{1,0:T(8,128)(2,1)} %bitcast.5, bf16[128,2048]{1,0:T(8,128)(2,1)} %bitcast.6, bf16[128,2048]{1,0:T(8,128)(2,1)} %bitcast.7, f32[5,1,2048]{2,1,0:T(1,128)} %bitcast.8), custom_call_target="tpu_custom_call" | custom-call | tf_op jit(solution)/shard_map/section_backward/pallas_call | solution.py:503
  116.7 1.9 %copy.5 = bf16[1,8,16,2048]{3,2,1,0:T(8,128)(2,1)} copy(bf16[1,8,16,2048]{3,2,1,0:T(8,128)(2,1)} %bitcast.4) | data formatting | bytes 1048576

commit v6 on v5

--- a/solution.py
+++ b/solution.py
@@ -286,7 +286,11 @@
             for index, share in enumerate(shares):
                 scale_ref[row, index : index + 1, :] = share * inverse
 
-        loop(0, rows, soften)
+        def soften_pair(turn):
+            soften(2 * turn)
+            soften(2 * turn + 1)
+
+        loop(0, rows // 2, soften_pair)
 
         def upstream(hop):
             src = back(hop)

time: 119 us -> 117 us (0.983)
  Pallas kernels: 117 us -> 115 us
    pallas_call x1, Pallas kernels: 117 us -> 115 us  [per_device(): pl.pallas_call(section_kernel, out_shape=jax.ShapeDtypeStruct((area, widt...]
where the time goes in v6:
time: 117 us
  Pallas kernels  115 us (98%)
  local copies, waits for them, and re-layouts  1.88 us (2%)
    pallas_call x1, Pallas kernels, per_device(): pl.pallas_call(section_kernel, out_shape=jax.ShapeDtypeStruct((area, widt...  115 us

profile of v6, /device:TPU:22, one launch (start us, length us, event | category | flops | bytes accessed | tf_op | source)
XLA Modules:
  0.0 117.1 jit_solution(6265476618226060376)
XLA Ops:
  0.0 115.2 %section_backward.1 = bf16[128,2048]{1,0:T(8,128)(2,1)} custom-call(bf16[128,2048]{1,0:T(8,128)(2,1)} %bitcast.5, bf16[128,2048]{1,0:T(8,128)(2,1)} %bitcast.6, bf16[128,2048]{1,0:T(8,128)(2,1)} %bitcast.7, f32[5,1,2048]{2,1,0:T(1,128)} %bitcast.8), custom_call_target="tpu_custom_call" | custom-call | tf_op jit(solution)/shard_map/section_backward/pallas_call | solution.py:507
  115.2 1.9 %copy.5 = bf16[1,8,16,2048]{3,2,1,0:T(8,128)(2,1)} copy(bf16[1,8,16,2048]{3,2,1,0:T(8,128)(2,1)} %bitcast.4) | data formatting | bytes 1048576
